TPU v7x, 32 devices: a whole 2x2x4 slice. The times are simulated.
32 devices in a mesh: dom: 2 (over y), row: 4 (over z), nbr: 4 (over x, core).
Axes of the slice: x: 2, y: 2, z: 4, core: 2. Of those that a mesh axis runs over, the one named last changes fastest.
Arguments:
- blocks: float32 [24, 12, 128, 128], P(('dom', 'row'), 'nbr'), parts along dimension 0, may hold values from -0.15625 to 0.15625
- partner_ids: int32 [24, 12], P(('dom', 'row'), 'nbr'), parts along dimension 0, may hold values from 0 to 11, as said below
- counts: int32 [24], P(('dom', 'row')), parts along dimension 0, may hold values from 1 to 12, as said below
- start: float32 [3072, 32], P(('dom', 'row')), parts along dimension 0, may hold values from -6 to 6
Outputs:
- basis: float32 [3072, 32], P(('dom', 'row')), parts along dimension 0
- ritz: float32 [64, 32], P('dom'), parts along dimension 0
There are 2 independent parts, one for each index of `dom`. A program takes and returns all parts, laid end to end along the dimension named above; each array names one. Nothing has to cross between parts.
Inputs may be any that keep to these rules, and one draw needn't show every extreme that they name: partner_ids[i,0] == i; slots 1 to counts[i] - 1 hold distinct block columns greater than i; slots from counts[i] on hold i. counts[i] <= min(12, 12 - i); counts[0] == 12.
All inputs are finite; a program needn't handle non-finite values.
Results may differ from a plain program's by a relative error of at most 0.0001.
Values sent between devices are 32-bit elements; how exact they have to be, the bound alone decides.
A program may use at most 64 MiB of HBM per device.

v0:
```python
import jax
import jax.numpy as jnp
from jax import lax
from jax.sharding import PartitionSpec as P

ITERS = 2


HIGH = lax.Precision.HIGHEST


def orthonormal(image, gram, total):
    lower = jnp.linalg.cholesky(gram / total)
    return lax.linalg.triangular_solve(lower, image, left_side=False, lower=True, transpose_a=True)


def body(blocks, partner_ids, counts, start):
    block_rows, slots_here = partner_ids.shape
    block_size = blocks.shape[2]
    columns = start.shape[1]
    row_count = lax.axis_size("row")
    all_blocks = block_rows * row_count
    total = all_blocks * block_size
    first_row = lax.axis_index("row") * block_rows
    rows_here = first_row + jnp.arange(block_rows, dtype=jnp.int32)
    slot_index = lax.axis_index("nbr") * slots_here + jnp.arange(slots_here, dtype=jnp.int32)
    valid = slot_index[None, :] < counts[:, None]
    weight = jnp.where(valid, jnp.where(partner_ids == rows_here[:, None], 0.5, 1.0), 0.0).astype(
        jnp.float32
    )
    targets = jnp.concatenate([partner_ids.reshape(-1), rows_here])
    whole = lax.all_gather(start, "row", axis=0, tiled=True)
    cross = jnp.zeros((columns, columns), jnp.float32)
    prior = start
    for step in range(ITERS):
        tiles = whole.reshape(all_blocks, block_size, columns)
        far = tiles[partner_ids] * weight[:, :, None, None]
        near = lax.dynamic_slice_in_dim(tiles, first_row, block_rows, 0)
        direct = jnp.einsum("ipab,ipbk->iak", blocks, far, precision=HIGH)
        transposed = (
            jnp.einsum("ipab,iak->ipbk", blocks, near, precision=HIGH) * weight[:, :, None, None]
        )
        items = jnp.concatenate(
            [transposed.reshape(block_rows * slots_here, block_size, columns), direct], axis=0
        )
        placed = jnp.zeros((all_blocks, block_size, columns), jnp.float32).at[targets].add(items)
        summed = lax.psum_scatter(
            placed.reshape(total, columns), "row", scatter_dimension=0, tiled=True
        )
        image = lax.psum(summed, "nbr")
        gram, cross = lax.psum(
            (jnp.dot(image.T, image, precision=HIGH), jnp.dot(prior.T, image, precision=HIGH)),
            "row",
        )
        cross = cross / total
        prior = orthonormal(image, gram, total)
        if step + 1 < ITERS:
            whole = lax.all_gather(prior, "row", axis=0, tiled=True)
    return (prior, cross)


def solution(mesh):
    return jax.shard_map(
        body,
        mesh=mesh,
        in_specs=(
            P(("dom", "row"), "nbr", None, None),
            P(("dom", "row"), "nbr"),
            P(("dom", "row")),
            P(("dom", "row"), None),
        ),
        out_specs=(P(("dom", "row"), None), P("dom", None)),
        check_vma=False,
    )
```

profile of v0, /device:TPU:0, one launch (start us, length us, event | category | flops | bytes accessed | tf_op | source)
XLA Modules:
  0.0 162.4 jit_solution(3839742283190382437)
XLA Ops:
  7.2 0.8 concatenate.32
  8.2 15.7 %all_gather.6 = f32[1536,32]{0,1:T(8,128)S(1)} all-gather(f32[384,32]{0,1:T(8,128)} %param.10), channel_id=1, replica_groups=mesh['dom'=2,'row'=4,'nbr'=4] {'row'}, dimensions={0}, use_global_device_ids=true | all-gather | bytes 245760 | tf_op jit(solution)/shard_map/all_gather | solution.py:32
  23.9 0.6 gather_fusion
  24.4 0.6 copy-done.2
  25.2 0.5 convolution_multiply_fusion.1
  25.6 0.8 convolution_bitcast_fusion.3
  26.5 1.1 scatter_fusion
  27.6 0.7 copy_bitcast_fusion.1
  28.4 21.0 %reduce-scatter.3.cloned.1.call-done = f32[384,32]{0,1:T(8,128)} async-done(((f32[1536,32]{0,1:T(8,128)}), f32[384,32]{0,1:T(8,128)}) %reduce-scatter.3.cloned.1.call-update) | async-done | bytes 49168 | tf_op jit(solution)/shard_map/reduce_scatter | solution.py:47
  49.4 11.0 %psum.35 = f32[384,32]{0,1:T(8,128)S(1)} all-reduce(f32[384,32]{0,1:T(8,128)} %reduce-scatter.3.cloned.1.call-done), channel_id=1, replica_groups=mesh['dom'=2,'row'=4,'nbr'=4] {'nbr'}, use_global_device_ids=true, to_apply=%region_2.3 | all-reduce | flops 12288 | bytes 98304 | tf_op jit(solution)/shard_map/psum | solution.py:50
  60.6 15.8 %psum.36 = f32[32,32]{0,1:T(8,128)S(1)} all-reduce(f32[32,32]{0,1:T(8,128)S(1)} %fusion.20), channel_id=1, replica_groups=mesh['dom'=2,'row'=4,'nbr'=4] {'row'}, use_global_device_ids=true, to_apply=%region_3.4 | all-reduce | flops 1024 | bytes 8192 | tf_op jit(solution)/shard_map/psum | solution.py:51
  76.5 2.9 %cholesky.44 = f32[32,32]{1,0:T(8,128)S(1)} custom-call(f32[32,32]{1,0:T(8,128)S(1)} %fusion.13), custom_call_target="Cholesky" | custom-call | tf_op jit(solution)/shard_map/jit(cholesky)/cholesky | solution.py:13
  79.5 0.6 compare_reduce_fusion.1
  80.1 0.7 fusion.8
  80.8 2.4 %custom-call.6 = f32[1,32,32]{1,2,0:T(8,128)S(1)} custom-call(f32[1,32,32]{2,1,0:T(8,128)S(1)} %fusion.8), custom_call_target="InvertDiagBlocksLowerTriangular" | custom-call | tf_op jit(solution)/shard_map/triangular_solve/custom-call.0 | solution.py:14
  83.2 0.3 convolution_bitcast_fusion.2
  83.5 13.6 %all_gather.7 = f32[1536,32]{0,1:T(8,128)S(1)} all-gather(f32[384,32]{0,1:T(8,128)S(1)} %convolution_bitcast_fusion.2), channel_id=1, replica_groups=mesh['dom'=2,'row'=4,'nbr'=4] {'row'}, dimensions={0}, use_global_device_ids=true | all-gather | bytes 245760 | tf_op jit(solution)/shard_map/all_gather | solution.py:58
  97.1 0.6 gather_fusion.1
  97.6 0.5 convolution_multiply_fusion
  98.1 0.8 convolution_bitcast_fusion.1
  98.9 1.1 scatter_fusion.1
  100.0 0.7 copy_bitcast_fusion
  100.7 18.9 %reduce-scatter.5.cloned.1.call-done = f32[384,32]{0,1:T(8,128)} async-done(((f32[1536,32]{0,1:T(8,128)}), f32[384,32]{0,1:T(8,128)}) %reduce-scatter.5.cloned.1.call-update) | async-done | bytes 49168 | tf_op jit(solution)/shard_map/reduce_scatter | solution.py:47
  119.6 11.0 %psum.37 = f32[384,32]{0,1:T(8,128)S(1)} all-reduce(f32[384,32]{0,1:T(8,128)} %reduce-scatter.5.cloned.1.call-done), channel_id=1, replica_groups=mesh['dom'=2,'row'=4,'nbr'=4] {'nbr'}, use_global_device_ids=true, to_apply=%region_8.11 | all-reduce | flops 12288 | bytes 98304 | tf_op jit(solution)/shard_map/psum | solution.py:50
  130.6 0.2 fusion.22
  131.0 16.2 %all-reduce = (f32[32,32]{0,1:T(8,128)S(1)}, f32[32,32]{0,1:T(8,128)S(1)}) all-reduce(f32[32,32]{0,1:T(8,128)S(1)} %fusion.21, f32[32,32]{0,1:T(8,128)S(1)} %fusion.22), channel_id=1, replica_groups=mesh['dom'=2,'row'=4,'nbr'=4] {'row'}, use_global_device_ids=true, to_apply=%region_9.12 | all-reduce | flops 2048 | bytes 16384 | tf_op jit(solution)/shard_map/psum | solution.py:51
  147.2 0.7 copy.37
  148.0 2.9 %cholesky.55 = f32[32,32]{1,0:T(8,128)S(1)} custom-call(f32[32,32]{1,0:T(8,128)S(1)} %fusion.11), custom_call_target="Cholesky" | custom-call | tf_op jit(solution)/shard_map/jit(cholesky)/cholesky | solution.py:13
  150.9 0.6 compare_reduce_fusion
  151.6 0.7 fusion.9
  152.2 2.4 %custom-call.7 = f32[1,32,32]{1,2,0:T(8,128)S(1)} custom-call(f32[1,32,32]{2,1,0:T(8,128)S(1)} %fusion.9), custom_call_target="InvertDiagBlocksLowerTriangular" | custom-call | tf_op jit(solution)/shard_map/triangular_solve/custom-call.0 | solution.py:14
  154.7 0.9 convolution_bitcast_fusion
  (33 shorter events, 1.1 us)
Async XLA Ops:
  7.2 18.0 %copy-start = (f32[3,3,128,128]{3,2,1,0:T(8,128)S(1)}, f32[3,3,128,128]{3,2,1,0:T(8,128)}, u32[]{:S(2)}) copy-start(f32[3,3,128,128]{3,2,1,0:T(8,128)} %param.7) | copy-start | bytes 1769476
  7.2 0.9 copy-start.1
  7.2 42.2 %reduce-scatter.3.cloned.1.call-start = ((), (), s32[]{:S(2)}) async-start(), calls=%async_computation.2 | async-start | bytes 245760 | tf_op jit(solution)/shard_map/reduce_scatter | solution.py:47
  24.4 0.7 copy-start.2
  28.3 91.3 %reduce-scatter.5.cloned.1.call-start = ((), (), s32[]{:S(2)}) async-start(), calls=%async_computation.3 | async-start | bytes 245760 | tf_op jit(solution)/shard_map/reduce_scatter | solution.py:47
Sparse Core Ops, SparseCore 0:
  28.4 20.9 reduce-scatter.2
  100.8 18.7 reduce-scatter.4
where the time goes:
time: 163 us; the launch traced here: 162 us
  blocking collectives  83.3 us (51%)
  waiting for transfers between devices  39.9 us (24%)
  other arithmetic  15.8 us (10%)
  between operations  14.3 us (9%)
  local copies, waits for them, and re-layouts  4.93 us (3%)
  matrix products  4.18 us (3%)
    reduce_scatter x2, waiting for transfers between devices, body(): lax.psum_scatter(placed.reshape(total, columns), 'row', scatter_dimension...  39.9 us
    psum x2, blocking collectives, body(): lax.psum((jnp.dot(image.T, image, precision=HIGH), jnp.dot(prior.T, image...  32 us
    psum x2, blocking collectives, body(): image = lax.psum(summed, 'nbr')  22 us
    all_gather x1, blocking collectives, body(): whole = lax.all_gather(start, 'row', axis=0, tiled=True)  15.7 us
    all_gather x1, blocking collectives, body(): whole = lax.all_gather(prior, 'row', axis=0, tiled=True)  13.6 us
    another operation x6, other arithmetic, orthonormal(): lower = jnp.linalg.cholesky(gram / total)  7.19 us
    another operation x4, other arithmetic, orthonormal(): lax.linalg.triangular_solve(lower, image, left_side=False, lower=True, tr...  6.17 us
  transfers between devices with their start and end apart: 2, of which 2 were waited for; matrix products, arithmetic and copies ran while one was open for 0% of the time, Pallas kernels for 0%

commit v1 on v0

--- a/solution.py
+++ b/solution.py
@@ -1,12 +1,18 @@
+import functools
+
 import jax
 import jax.numpy as jnp
 from jax import lax
+from jax.experimental import pallas as pl
+from jax.experimental.pallas import tpu as pltpu
 from jax.sharding import PartitionSpec as P
 
 ITERS = 2
-
+DIRECT_PEERS = 16
 
 HIGH = lax.Precision.HIGHEST
+F32 = jnp.float32
+BF16 = jnp.bfloat16
 
 
 def orthonormal(image, gram, total):
@@ -59,9 +65,345 @@
     return (prior, cross)
 
 
+def split(x):
+    high = x.astype(BF16)
+    return high, (x - high.astype(F32)).astype(BF16)
+
+
+def dot_nt(a, b):
+    return lax.dot_general(a, b, (((1,), (1,)), ((), ())), precision=HIGH, preferred_element_type=F32)
+
+
+def dot_nn(a, b, precision=HIGH):
+    return lax.dot_general(
+        a, b, (((1,), (0,)), ((), ())), precision=precision, preferred_element_type=F32
+    )
+
+
+def inverse_factor(gram_at, columns, lanes):
+    row = lax.broadcasted_iota(jnp.int32, (columns, lanes), 0)
+    lane = lax.broadcasted_iota(jnp.int32, (columns, lanes), 1)
+    work = jnp.where(lane < columns, jnp.where(lane == row, 1.0, 0.0), gram_at)
+    work = jnp.where(lane < 2 * columns, work, 0.0)
+    for k in range(columns):
+        pivot = work[k : k + 1, :]
+        at = columns + k
+        inverse = 1.0 / pivot[:, at : at + 1]
+        factor = jnp.where(row[:, :1] > k, work[:, at : at + 1] * inverse, 0.0)
+        work = work - factor * pivot
+    diagonal = jnp.sum(jnp.where(lane == row + columns, work, 0.0), axis=1, keepdims=True)
+    return (work * (1.0 / jnp.sqrt(diagonal)))[:, :columns]
+
+
+def kernel(
+    rows, nbrs, ids_ref, counts_ref, start_ref, blocks_ref, basis_ref, ritz_ref,
+    held, straight, turned, sel, weight, whole, part, inbox, stats, stats_in, images,
+    blocks_sem, start_send, start_recv, rs_send, rs_recv, ag_send, ag_recv,
+    st_send, st_recv, im_send, im_recv,
+):
+    block_rows, slots = ids_ref.shape
+    columns = start_ref.shape[0]
+    size = blocks_ref.shape[2]
+    tiles = block_rows * rows
+    total = tiles * size
+    group = rows * nbrs
+    my_row, my_nbr = lax.axis_index("row"), lax.axis_index("nbr")
+    me = my_row * nbrs + my_nbr
+    owner = my_nbr < block_rows
+    my_tile = my_row * block_rows + lax.min(my_nbr, block_rows - 1)
+
+    def place(d):
+        peer = lax.rem(me + d, group)
+        return peer // nbrs, lax.rem(peer, nbrs)
+
+    def device(r, n):
+        return {"row": r, "nbr": n}
+
+    barrier = pltpu.get_barrier_semaphore()
+    for d in range(1, group):
+        r, n = place(d)
+        pl.semaphore_signal(
+            barrier, inc=1, device_id=device(r, n), device_id_type=pl.DeviceIdType.MESH
+        )
+    load = pltpu.make_async_copy(blocks_ref, held, blocks_sem)
+    load.start()
+    for i in range(block_rows):
+        whole[0, my_row * block_rows + i] = start_ref[:, i * size : (i + 1) * size]
+    for i in range(block_rows):
+        for p in range(slots):
+            j = ids_ref[i, p]
+            valid = my_nbr * slots + p < counts_ref[i]
+            c = jnp.where(valid, jnp.where(j == my_row * block_rows + i, 0.5, 1.0), 0.0)
+            weight[i * slots + p] = c
+            for t in range(tiles):
+                sel[(i * slots + p) * tiles + t] = jnp.where(j == t, c, 0.0)
+    pl.semaphore_wait(barrier, group - 1)
+
+    def start_copy(d, i):
+        r = lax.rem(my_row + d, rows)
+        return pltpu.make_async_remote_copy(
+            src_ref=start_ref.at[:, pl.ds(i * size, size)],
+            dst_ref=whole.at[0, my_row * block_rows + i],
+            send_sem=start_send.at[d - 1, i],
+            recv_sem=start_recv.at[d - 1, i],
+            device_id=device(r, my_nbr),
+            device_id_type=pl.DeviceIdType.MESH,
+        )
+
+    for d in range(1, rows):
+        for i in range(block_rows):
+            start_copy(d, i).start()
+
+    load.wait()
+    span = slots * size
+    for i in range(block_rows):
+        for p in range(slots):
+            block = held[i, p]
+            high, low = split(block)
+            straight[i, :size, p * size : (p + 1) * size] = high
+            straight[i, size:, p * size : (p + 1) * size] = low
+            high, low = split(block.T)
+            turned[i, p * size : (p + 1) * size, :] = high
+            turned[i, span + p * size : span + (p + 1) * size, :] = low
+
+    for d in range(1, rows):
+        for i in range(block_rows):
+            start_copy(d, i).wait_recv()
+
+    def apply(step):
+        moved = []
+        for i in range(block_rows):
+            near = jnp.concatenate(split(whole[step, my_row * block_rows + i]), axis=0)
+            out = dot_nn(jnp.concatenate([near, near], axis=1), straight[i], None)
+            moved.append(out[:columns] + out[columns:])
+        for t in range(tiles):
+            summed = None
+            for i in range(block_rows):
+                for p in range(slots):
+                    term = moved[i][:, p * size : (p + 1) * size] * sel[(i * slots + p) * tiles + t]
+                    summed = term if summed is None else summed + term
+            part[step, t] = summed
+        for i in range(block_rows):
+            far = []
+            for p in range(slots):
+                tile = whole[step, ids_ref[i, p]] * weight[i * slots + p]
+                far.append(jnp.concatenate(split(tile), axis=0))
+            out = dot_nn(jnp.concatenate(far + far, axis=1), turned[i], None)
+            t = my_row * block_rows + i
+            part[step, t] = part[step, t] + (out[:columns] + out[columns:])
+
+    def sum_copy(step, d):
+        r, n = place(d)
+        return pltpu.make_async_remote_copy(
+            src_ref=part.at[step, r * block_rows + lax.min(n, block_rows - 1)],
+            dst_ref=inbox.at[step, d - 1],
+            send_sem=rs_send.at[step, d - 1],
+            recv_sem=rs_recv.at[step, d - 1],
+            device_id=device(r, n),
+            device_id_type=pl.DeviceIdType.MESH,
+        )
+
+    def send_sums(step):
+        for d in range(1, group):
+            @pl.when(place(d)[1] < block_rows)
+            def _():
+                sum_copy(step, d).start()
+
+    def gather_sums(step):
+        summed = part[step, my_tile]
+        for d in range(1, group):
+            sum_copy(step, d).wait_recv()
+            summed = summed + inbox[step, d - 1]
+        return summed
+
+    def image_copy(d):
+        r, n = place(d)
+        return pltpu.make_async_remote_copy(
+            src_ref=whole.at[1, my_tile],
+            dst_ref=whole.at[1, my_tile],
+            send_sem=ag_send.at[d - 1],
+            recv_sem=ag_recv.at[d - 1],
+            device_id=device(r, n),
+            device_id_type=pl.DeviceIdType.MESH,
+        )
+
+    def from_owner(d):
+        return lax.rem(me + group - d, nbrs) < block_rows
+
+    apply(0)
+    send_sums(0)
+
+    @pl.when(owner)
+    def _():
+        whole[1, my_tile] = gather_sums(0)
+        for d in range(1, group):
+            image_copy(d).start()
+
+    for d in range(1, group):
+        @pl.when(from_owner(d))
+        def _():
+            image_copy(d).wait_recv()
+
+    apply(1)
+    send_sums(1)
+
+    gram = jnp.zeros((columns, size), F32)
+    blank = jnp.zeros((columns, size), F32)
+    for t in range(tiles):
+        tile = whole[1, t]
+        gram = gram + dot_nt(tile, jnp.concatenate([blank, tile, blank, blank], axis=0))
+    first = inverse_factor(gram / total, columns, size)
+
+    def stats_copy(d):
+        r, n = place(d)
+        return pltpu.make_async_remote_copy(
+            src_ref=stats,
+            dst_ref=stats_in.at[d - 1],
+            send_sem=st_send.at[d - 1],
+            recv_sem=st_recv.at[d - 1],
+            device_id=device(r, n),
+            device_id_type=pl.DeviceIdType.MESH,
+        )
+
+    def own_copy(d):
+        return pltpu.make_async_remote_copy(
+            src_ref=images.at[lax.min(my_nbr, block_rows - 1)],
+            dst_ref=images.at[lax.min(my_nbr, block_rows - 1)],
+            send_sem=im_send.at[d - 1],
+            recv_sem=im_recv.at[d - 1],
+            device_id=device(my_row, lax.rem(my_nbr + d, nbrs)),
+            device_id_type=pl.DeviceIdType.MESH,
+        )
+
+    def own_from(d):
+        return lax.rem(my_nbr + nbrs - d, nbrs) < block_rows
+
+    half = columns // 2
+
+    @pl.when(owner)
+    def _():
+        prior = dot_nn(first, whole[1, my_tile])
+        image = dot_nn(first, gather_sums(1))
+        images[my_nbr] = image
+        both = dot_nt(image, jnp.concatenate([image, blank, blank, blank], axis=0))
+        other = dot_nt(prior, jnp.concatenate([blank, image, blank, blank], axis=0))
+        both = both + other
+        stats[...] = both[:half] + pltpu.roll(both[half:], 2 * columns, 1)
+        for d in range(1, group):
+            stats_copy(d).start()
+        for d in range(1, nbrs):
+            own_copy(d).start()
+
+    @pl.when(jnp.logical_not(owner))
+    def _():
+        stats[...] = jnp.zeros_like(stats)
+
+    stats_in[group - 1] = stats[...]
+    for d in range(1, group):
+        @pl.when(from_owner(d))
+        def _():
+            stats_copy(d).wait_recv()
+
+        @pl.when(jnp.logical_not(from_owner(d)))
+        def _():
+            stats_in[d - 1] = jnp.zeros_like(stats)
+
+    packed = stats_in[group - 1]
+    for d in range(1, group):
+        packed = packed + stats_in[d - 1]
+    packed = packed / total
+    rest = jnp.concatenate([packed, pltpu.roll(packed, 2 * columns, 1)], axis=0)
+    last = inverse_factor(pltpu.roll(rest, columns, 1), columns, size)
+    ritz_ref[...] = pltpu.roll(rest, size - columns, 1)[:, :columns]
+    for d in range(1, nbrs):
+        @pl.when(own_from(d))
+        def _():
+            own_copy(d).wait_recv()
+    for i in range(block_rows):
+        basis_ref[:, i * size : (i + 1) * size] = dot_nn(last, images[i])
+
+    for d in range(1, rows):
+        for i in range(block_rows):
+            start_copy(d, i).wait_send()
+    for step in range(ITERS):
+        for d in range(1, group):
+            @pl.when(place(d)[1] < block_rows)
+            def _():
+                sum_copy(step, d).wait_send()
+
+    @pl.when(owner)
+    def _():
+        for d in range(1, group):
+            image_copy(d).wait_send()
+            stats_copy(d).wait_send()
+        for d in range(1, nbrs):
+            own_copy(d).wait_send()
+
+
+def direct_body(rows, nbrs, blocks, partner_ids, counts, start):
+    block_rows, slots = partner_ids.shape
+    size = blocks.shape[2]
+    columns = start.shape[1]
+    tiles = block_rows * rows
+    group = rows * nbrs
+    dma = pltpu.SemaphoreType.DMA
+    basis, ritz = pl.pallas_call(
+        functools.partial(kernel, rows, nbrs),
+        out_shape=(
+            jax.ShapeDtypeStruct((columns, block_rows * size), F32),
+            jax.ShapeDtypeStruct((columns, columns), F32),
+        ),
+        in_specs=[
+            pl.BlockSpec(memory_space=pltpu.SMEM),
+            pl.BlockSpec(memory_space=pltpu.SMEM),
+            pl.BlockSpec(memory_space=pltpu.VMEM),
+            pl.BlockSpec(memory_space=pl.ANY),
+        ],
+        out_specs=(
+            pl.BlockSpec(memory_space=pltpu.VMEM),
+            pl.BlockSpec(memory_space=pltpu.VMEM),
+        ),
+        scratch_shapes=[
+            pltpu.VMEM((block_rows, slots, size, size), F32),
+            pltpu.VMEM((block_rows, 2 * size, slots * size), BF16),
+            pltpu.VMEM((block_rows, 2 * slots * size, size), BF16),
+            pltpu.SMEM((block_rows * slots * tiles,), F32),
+            pltpu.SMEM((block_rows * slots,), F32),
+            pltpu.VMEM((2, tiles, columns, size), F32),
+            pltpu.VMEM((2, tiles, columns, size), F32),
+            pltpu.VMEM((2, group - 1, columns, size), F32),
+            pltpu.VMEM((columns // 2, size), F32),
+            pltpu.VMEM((group, columns // 2, size), F32),
+            pltpu.VMEM((block_rows, columns, size), F32),
+            dma,
+            dma((rows - 1, block_rows)),
+            dma((rows - 1, block_rows)),
+            dma((2, group - 1)),
+            dma((2, group - 1)),
+            dma((group - 1,)),
+            dma((group - 1,)),
+            dma((group - 1,)),
+            dma((group - 1,)),
+            dma((nbrs - 1,)),
+            dma((nbrs - 1,)),
+        ],
+        compiler_params=pltpu.CompilerParams(collective_id=0, has_side_effects=True),
+    )(partner_ids, counts, start.T, blocks)
+    return basis.T, ritz
+
+
 def solution(mesh):
+    rows, nbrs = mesh.shape["row"], mesh.shape["nbr"]
+
+    def program(blocks, partner_ids, counts, start):
+        block_rows = partner_ids.shape[0]
+        size, columns = blocks.shape[2], start.shape[1]
+        if rows * nbrs <= DIRECT_PEERS and block_rows <= nbrs and size == 128 and 4 * columns == size:
+            return direct_body(rows, nbrs, blocks, partner_ids, counts, start)
+        return body(blocks, partner_ids, counts, start)
+
     return jax.shard_map(
-        body,
+        program,
         mesh=mesh,
         in_specs=(
             P(("dom", "row"), "nbr", None, None),

time: 163 us -> 44.9 us (0.28)
  blocking collectives: 83.3 us -> 0 us
  Pallas kernels: 0 us -> 42 us
  waiting for transfers between devices: 39.9 us -> 0 us
  other arithmetic: 15.8 us -> 0 us
  between operations: 14.3 us -> 0.65 us
  matrix products: 4.18 us -> 0 us
  local copies, waits for them, and re-layouts: 4.93 us -> 2.04 us
    psum x4 -> x0, blocking collectives: 54 us -> none  [the longest x2 32 us: body(): lax.psum((jnp.dot(image.T, image, precision=HIGH), jnp.dot(prior.T, image...]
    pallas_call x0 -> x1, Pallas kernels: none -> 42 us  [direct_body(): pl.pallas_call(functools.partial(kernel, rows, nbrs), out_shape=(jax.Shap...]
    reduce_scatter x2 -> x0, waiting for transfers between devices: 39.9 us -> none  [body(): lax.psum_scatter(placed.reshape(total, columns), 'row', scatter_dimension...]
    all_gather x2 -> x0, blocking collectives: 29.2 us -> none  [the longest x1 15.7 us: body(): whole = lax.all_gather(start, 'row', axis=0, tiled=True)]
    another operation x10 -> x0, other arithmetic: 13.4 us -> none  [the longest x6 7.19 us: orthonormal(): lower = jnp.linalg.cholesky(gram / total)]
    dot_general x7 -> x0, matrix products: 3.01 us -> none  [the longest x2 1.5 us: body(): direct = jnp.einsum('ipab,ipbk->iak', blocks, far, precision=HIGH)]
    scatter-add x2 -> x0, other arithmetic: 2.15 us -> none  [body(): jnp.zeros((all_blocks, block_size, columns), jnp.float32).at[targets]]
  transfers between devices with their start and end apart: 2 -> 0, of which waited for: 2 -> 0; matrix products, arithmetic and copies ran while one was open for 0% -> 0% of each run, Pallas kernels for 0% -> 0%
where the time goes in v1:
time: 44.9 us; the launch traced here: 44.7 us
  Pallas kernels  42 us (94%)
  local copies, waits for them, and re-layouts  2.04 us (5%)
  between operations  0.65 us (1%)
    pallas_call x1, Pallas kernels, direct_body(): pl.pallas_call(functools.partial(kernel, rows, nbrs), out_shape=(jax.Shap...  42 us
    unnamed x4, local copies, waits for them, and re-layouts  2.04 us

profile of v1, /device:TPU:0, one launch (start us, length us, event | category | flops | bytes accessed | tf_op | source)
XLA Modules:
  0.0 44.7 jit_solution(7273258604824492345)
XLA Ops:
  0.6 42.0 %shard_map.59 = (f32[32,384]{1,0:T(8,128)}, f32[32,32]{1,0:T(8,128)}) custom-call(s32[3,3]{1,0:T(4,128)} %ids_ref.1, s32[3]{0:T(128)} %counts_ref.1, f32[32,384]{1,0:T(8,128)} %bitcast.2, f32[3,3,128,128]{3,2,1,0:T(8,128)} %blocks_ref.1), custom_call_target="tpu_custom_call" | custom-call | tf_op jit(solution)/shard_map/pallas_call | solution.py:350
  42.7 0.0 copy-start
  42.7 1.4 %copy.8 = f32[384,32]{0,1:T(8,128)} copy(f32[384,32]{0,1:T(8,128)} %bitcast.3) | data formatting | bytes 98304
  44.1 0.0 copy-done
  44.1 0.6 %copy.9 = f32[32,32]{1,0:T(8,128)} copy(f32[32,32]{1,0:T(8,128)S(1)} %copy-done) | data formatting | bytes 8192
Async XLA Ops:
  42.7 1.4 %copy-start = (f32[32,32]{1,0:T(8,128)S(1)}, f32[32,32]{1,0:T(8,128)}, u32[]{:S(2)}) copy-start(f32[32,32]{1,0:T(8,128)} %get-tuple-element.9) | copy-start | bytes 12292

commit v2 on v1

v2 whole, which is shorter than its diff:
```python
import functools

import jax
import jax.numpy as jnp
from jax import lax
from jax.experimental import pallas as pl
from jax.experimental.pallas import tpu as pltpu
from jax.sharding import PartitionSpec as P

ITERS = 2
DIRECT_PEERS = 16

HIGH = lax.Precision.HIGHEST
F32 = jnp.float32
BF16 = jnp.bfloat16


def orthonormal(image, gram, total):
    lower = jnp.linalg.cholesky(gram / total)
    return lax.linalg.triangular_solve(lower, image, left_side=False, lower=True, transpose_a=True)


def body(blocks, partner_ids, counts, start):
    block_rows, slots_here = partner_ids.shape
    block_size = blocks.shape[2]
    columns = start.shape[1]
    row_count = lax.axis_size("row")
    all_blocks = block_rows * row_count
    total = all_blocks * block_size
    first_row = lax.axis_index("row") * block_rows
    rows_here = first_row + jnp.arange(block_rows, dtype=jnp.int32)
    slot_index = lax.axis_index("nbr") * slots_here + jnp.arange(slots_here, dtype=jnp.int32)
    valid = slot_index[None, :] < counts[:, None]
    weight = jnp.where(valid, jnp.where(partner_ids == rows_here[:, None], 0.5, 1.0), 0.0).astype(
        jnp.float32
    )
    targets = jnp.concatenate([partner_ids.reshape(-1), rows_here])
    whole = lax.all_gather(start, "row", axis=0, tiled=True)
    cross = jnp.zeros((columns, columns), jnp.float32)
    prior = start
    for step in range(ITERS):
        tiles = whole.reshape(all_blocks, block_size, columns)
        far = tiles[partner_ids] * weight[:, :, None, None]
        near = lax.dynamic_slice_in_dim(tiles, first_row, block_rows, 0)
        direct = jnp.einsum("ipab,ipbk->iak", blocks, far, precision=HIGH)
        transposed = (
            jnp.einsum("ipab,iak->ipbk", blocks, near, precision=HIGH) * weight[:, :, None, None]
        )
        items = jnp.concatenate(
            [transposed.reshape(block_rows * slots_here, block_size, columns), direct], axis=0
        )
        placed = jnp.zeros((all_blocks, block_size, columns), jnp.float32).at[targets].add(items)
        summed = lax.psum_scatter(
            placed.reshape(total, columns), "row", scatter_dimension=0, tiled=True
        )
        image = lax.psum(summed, "nbr")
        gram, cross = lax.psum(
            (jnp.dot(image.T, image, precision=HIGH), jnp.dot(prior.T, image, precision=HIGH)),
            "row",
        )
        cross = cross / total
        prior = orthonormal(image, gram, total)
        if step + 1 < ITERS:
            whole = lax.all_gather(prior, "row", axis=0, tiled=True)
    return (prior, cross)


def split(x):
    high = x.astype(BF16)
    return high, (x - high.astype(F32)).astype(BF16)


def dot_nt(a, b):
    return lax.dot_general(a, b, (((1,), (1,)), ((), ())), precision=HIGH, preferred_element_type=F32)


def dot_nn(a, b, precision=HIGH):
    return lax.dot_general(
        a, b, (((1,), (0,)), ((), ())), precision=precision, preferred_element_type=F32
    )


def inverse_factor(gram_at, columns, lanes):
    row = lax.broadcasted_iota(jnp.int32, (columns, lanes), 0)
    lane = lax.broadcasted_iota(jnp.int32, (columns, lanes), 1)
    work = jnp.where(lane < columns, jnp.where(lane == row, 1.0, 0.0), gram_at)
    work = jnp.where(lane < 2 * columns, work, 0.0)
    for k in range(columns):
        pivot = work[k : k + 1, :]
        at = columns + k
        inverse = 1.0 / pivot[:, at : at + 1]
        factor = jnp.where(row[:, :1] > k, work[:, at : at + 1] * inverse, 0.0)
        work = work - factor * pivot
    diagonal = jnp.sum(jnp.where(lane == row + columns, work, 0.0), axis=1, keepdims=True)
    return (work * (1.0 / jnp.sqrt(diagonal)))[:, :columns]


def kernel(
    rows, nbrs, ids_ref, counts_ref, start_ref, blocks_ref, basis_ref, ritz_ref,
    held, straight, turned, sel, weight, begun, first_image, part, inbox, near_part, near_inbox, total_sum,
    grams, stats, images,
    blocks_sem, start_send, start_recv, rs_send, rs_recv, near_send, near_recv, ag_send, ag_recv,
    gram_send, gram_recv, st_send, st_recv, im_send, im_recv,
):
    block_rows, slots = ids_ref.shape
    columns = start_ref.shape[0]
    size = blocks_ref.shape[2]
    tiles = block_rows * rows
    total = tiles * size
    group = rows * nbrs
    my_row, my_nbr = lax.axis_index("row"), lax.axis_index("nbr")
    me = my_row * nbrs + my_nbr
    owner = my_nbr < block_rows
    my_slot = lax.min(my_nbr, block_rows - 1)
    first_tile = my_row * block_rows
    my_tile = first_tile + my_slot
    whole = (begun, first_image)
    blank = jnp.zeros((columns, size), F32)

    def send(src, dst, send_sem, recv_sem, r, n):
        return pltpu.make_async_remote_copy(
            src_ref=src, dst_ref=dst, send_sem=send_sem, recv_sem=recv_sem,
            device_id={"row": r, "nbr": n}, device_id_type=pl.DeviceIdType.MESH,
        )

    barrier = pltpu.get_barrier_semaphore()
    for d in range(1, group):
        peer = lax.rem(me + d, group)
        pl.semaphore_signal(
            barrier, inc=1, device_id={"row": peer // nbrs, "nbr": lax.rem(peer, nbrs)},
            device_id_type=pl.DeviceIdType.MESH,
        )
    load = pltpu.make_async_copy(blocks_ref, held, blocks_sem)
    load.start()
    for i in range(block_rows):
        begun[first_tile + i] = start_ref[:, i * size : (i + 1) * size]
    for q in range(rows - 1):
        @pl.when(q < my_row)
        def _():
            for i in range(block_rows):
                begun[q * block_rows + i] = blank
                first_image[q * block_rows + i] = blank
    for i in range(block_rows):
        for p in range(slots):
            j = ids_ref[i, p]
            valid = my_nbr * slots + p < counts_ref[i]
            c = jnp.where(valid, jnp.where(j == first_tile + i, 0.5, 1.0), 0.0)
            weight[i * slots + p] = c
            for t in range(tiles):
                sel[(i * slots + p) * tiles + t] = jnp.where(j == t, c, 0.0)

    load.wait()
    span = slots * size
    for i in range(block_rows):
        for p in range(slots):
            block = held[i, p]
            high, low = split(block)
            straight[i, :size, p * size : (p + 1) * size] = high
            straight[i, size:, p * size : (p + 1) * size] = low
            high, low = split(block.T)
            turned[i, p * size : (p + 1) * size, :] = high
            turned[i, span + p * size : span + (p + 1) * size, :] = low

    def transposed(step):
        moved = []
        for i in range(block_rows):
            near = jnp.concatenate(split(whole[step][first_tile + i]), axis=0)
            out = dot_nn(jnp.concatenate([near, near], axis=1), straight[i], None)
            moved.append(out[:columns] + out[columns:])
        for t in range(tiles):
            summed = None
            for i in range(block_rows):
                for p in range(slots):
                    term = moved[i][:, p * size : (p + 1) * size] * sel[(i * slots + p) * tiles + t]
                    summed = term if summed is None else summed + term
            part[step, t] = summed

    def direct(step):
        for i in range(block_rows):
            far = []
            for p in range(slots):
                tile = whole[step][ids_ref[i, p]] * weight[i * slots + p]
                far.append(jnp.concatenate(split(tile), axis=0))
            out = dot_nn(jnp.concatenate(far + far, axis=1), turned[i], None)
            near_part[step, i] = out[:columns] + out[columns:]

    def start_copy(q, i):
        return send(
            start_ref.at[:, pl.ds(i * size, size)], begun.at[first_tile + i],
            start_send.at[q, i], start_recv.at[my_row, i], q, my_nbr,
        )

    def start_wait(q, i):
        send(
            start_ref.at[:, pl.ds(i * size, size)], begun.at[q * block_rows + i],
            start_send.at[q, i], start_recv.at[q, i], q, my_nbr,
        ).wait_recv()

    def sum_copy(step, r, n):
        return send(
            part.at[step, r * block_rows + n], inbox.at[step, me],
            rs_send.at[step, r, n], rs_recv.at[step, me], r, n,
        )

    def sum_wait(step, r, n):
        send(
            part.at[step, my_tile], inbox.at[step, r * nbrs + n],
            rs_send.at[step, 0, 0], rs_recv.at[step, r * nbrs + n], r, n,
        ).wait_recv()

    def each_sum(step, act):
        for r in range(rows):
            for n in range(block_rows):
                @pl.when(jnp.logical_and(r >= my_row, r * nbrs + n != me))
                def _():
                    act(sum_copy(step, r, n))

    def near_copy(step, i):
        return send(
            near_part.at[step, i], near_inbox.at[step, my_nbr],
            near_send.at[step, i], near_recv.at[step, my_nbr], my_row, i,
        )

    def near_wait(step, n):
        send(
            near_part.at[step, my_slot], near_inbox.at[step, n],
            near_send.at[step, 0], near_recv.at[step, n], my_row, n,
        ).wait_recv()

    def each_near(step, act):
        for i in range(block_rows):
            @pl.when(i != my_nbr)
            def _():
                act(near_copy(step, i))

    def gather_sums(step):
        total_sum[...] = part[step, my_tile] + near_part[step, my_slot]
        for q in range(rows - 1):
            @pl.when(q < my_row)
            def _():
                for n in range(nbrs):
                    sum_wait(step, q, n)
                summed = inbox[step, q * nbrs]
                for n in range(1, nbrs):
                    summed = summed + inbox[step, q * nbrs + n]
                total_sum[...] += summed
        for e in range(1, nbrs):
            n = lax.rem(my_nbr + e, nbrs)
            sum_wait(step, my_row, n)
            total_sum[...] += inbox[step, my_row * nbrs + n]
        for e in range(1, nbrs):
            n = lax.rem(my_nbr + e, nbrs)
            near_wait(step, n)
            total_sum[...] += near_inbox[step, n]
        return total_sum[...]

    def image_copy(r, n):
        return send(
            first_image.at[my_tile], first_image.at[my_tile],
            ag_send.at[r, n], ag_recv.at[my_tile], r, n,
        )

    def image_wait(t):
        send(
            first_image.at[t], first_image.at[t], ag_send.at[0, 0], ag_recv.at[t], my_row, my_nbr
        ).wait_recv()

    def near_images(act):
        for e in range(1, nbrs):
            act(image_copy(my_row, lax.rem(my_nbr + e, nbrs)))

    def far_images(act):
        for q in range(rows - 1):
            @pl.when(q < my_row)
            def _():
                for n in range(nbrs):
                    act(image_copy(q, n))

    def gram_copy(t):
        return send(
            grams.at[my_tile], grams.at[my_tile],
            gram_send.at[t], gram_recv.at[my_tile], t // block_rows, t % block_rows,
        )

    def gram_wait(t):
        send(
            grams.at[t], grams.at[t], gram_send.at[t], gram_recv.at[t],
            t // block_rows, t % block_rows,
        ).wait_recv()

    def each_gram(act):
        for t in range(tiles):
            @pl.when(t != my_tile)
            def _():
                act(t)

    def stats_copy(g):
        return send(
            stats.at[my_tile], stats.at[my_tile],
            st_send.at[g], st_recv.at[my_tile], g // nbrs, g % nbrs,
        )

    def stats_wait(t):
        send(
            stats.at[t], stats.at[t], st_send.at[0], st_recv.at[t], my_row, my_nbr
        ).wait_recv()

    def each_stats(act):
        for g in range(group):
            @pl.when(g != me)
            def _():
                act(stats_copy(g))

    def own_copy(e):
        return send(
            images.at[my_slot], images.at[my_slot],
            im_send.at[e - 1], im_recv.at[my_slot], my_row, lax.rem(my_nbr + e, nbrs),
        )

    def own_wait(i):
        send(
            images.at[i], images.at[i], im_send.at[0], im_recv.at[i], my_row, my_nbr
        ).wait_recv()

    def each_start(act):
        for q in range(rows - 1):
            @pl.when(q < my_row)
            def _():
                for i in range(block_rows):
                    act(start_copy(q, i))

    def begin(copy):
        copy.start()

    def end(copy):
        copy.wait_send()

    transposed(0)
    pl.semaphore_wait(barrier, group - 1)
    each_start(begin)
    each_sum(0, begin)
    for q in range(1, rows):
        @pl.when(q > my_row)
        def _():
            for i in range(block_rows):
                start_wait(q, i)
    direct(0)
    each_near(0, begin)

    quarter, half = columns // 4, columns // 2

    @pl.when(owner)
    def _():
        tile = gather_sums(0)
        first_image[my_tile] = tile
        near_images(begin)
        far_images(begin)
        gram = dot_nt(tile, jnp.concatenate([tile, blank, blank, blank], axis=0))
        packed = gram[:quarter]
        for g in range(1, 4):
            packed = packed + pltpu.roll(gram[g * quarter : (g + 1) * quarter], g * columns, 1)
        grams[my_tile] = packed
        each_gram(lambda t: gram_copy(t).start())

    for i in range(block_rows):
        @pl.when(i != my_nbr)
        def _():
            image_wait(first_tile + i)
    transposed(1)
    each_sum(1, begin)
    for q in range(1, rows):
        @pl.when(q > my_row)
        def _():
            for i in range(block_rows):
                image_wait(q * block_rows + i)
    direct(1)
    each_near(1, begin)

    @pl.when(owner)
    def _():
        each_gram(gram_wait)
        packed = grams[0]
        for t in range(1, tiles):
            packed = packed + grams[t]
        packed = packed / total
        gram = jnp.concatenate(
            [pltpu.roll(packed, size - g * columns, 1) if g else packed for g in range(4)], axis=0
        )
        first = inverse_factor(pltpu.roll(gram, columns, 1), columns, size)
        prior = dot_nn(first, first_image[my_tile])
        image = dot_nn(first, gather_sums(1))
        images[my_nbr] = image
        both = dot_nt(image, jnp.concatenate([image, blank, blank, blank], axis=0))
        other = dot_nt(prior, jnp.concatenate([blank, image, blank, blank], axis=0))
        both = both + other
        stats[my_tile] = both[:half] + pltpu.roll(both[half:], 2 * columns, 1)
        each_stats(begin)
        for e in range(1, nbrs):
            own_copy(e).start()

    for t in range(tiles):
        @pl.when(jnp.logical_or(jnp.logical_not(owner), t != my_tile))
        def _():
            stats_wait(t)
    packed = stats[0]
    for t in range(1, tiles):
        packed = packed + stats[t]
    packed = packed / total
    rest = jnp.concatenate([packed, pltpu.roll(packed, 2 * columns, 1)], axis=0)
    last = inverse_factor(pltpu.roll(rest, columns, 1), columns, size)
    ritz_ref[...] = pltpu.roll(rest, size - columns, 1)[:, :columns]
    for i in range(block_rows):
        @pl.when(i != my_nbr)
        def _():
            own_wait(i)
    for i in range(block_rows):
        basis_ref[:, i * size : (i + 1) * size] = dot_nn(last, images[i])

    each_start(end)
    for step in range(ITERS):
        each_sum(step, end)
        each_near(step, end)

    @pl.when(owner)
    def _():
        near_images(end)
        far_images(end)
        each_gram(lambda t: gram_copy(t).wait_send())
        each_stats(end)
        for e in range(1, nbrs):
            own_copy(e).wait_send()


def direct_body(rows, nbrs, blocks, partner_ids, counts, start):
    block_rows, slots = partner_ids.shape
    size = blocks.shape[2]
    columns = start.shape[1]
    tiles = block_rows * rows
    group = rows * nbrs
    dma = pltpu.SemaphoreType.DMA
    basis, ritz = pl.pallas_call(
        functools.partial(kernel, rows, nbrs),
        out_shape=(
            jax.ShapeDtypeStruct((columns, block_rows * size), F32),
            jax.ShapeDtypeStruct((columns, columns), F32),
        ),
        in_specs=[
            pl.BlockSpec(memory_space=pltpu.SMEM),
            pl.BlockSpec(memory_space=pltpu.SMEM),
            pl.BlockSpec(memory_space=pltpu.VMEM),
            pl.BlockSpec(memory_space=pl.ANY),
        ],
        out_specs=(
            pl.BlockSpec(memory_space=pltpu.VMEM),
            pl.BlockSpec(memory_space=pltpu.VMEM),
        ),
        scratch_shapes=[
            pltpu.VMEM((block_rows, slots, size, size), F32),
            pltpu.VMEM((block_rows, 2 * size, slots * size), BF16),
            pltpu.VMEM((block_rows, 2 * slots * size, size), BF16),
            pltpu.SMEM((block_rows * slots * tiles,), F32),
            pltpu.SMEM((block_rows * slots,), F32),
            pltpu.VMEM((tiles, columns, size), F32),
            pltpu.VMEM((tiles, columns, size), F32),
            pltpu.VMEM((2, tiles, columns, size), F32),
            pltpu.VMEM((2, group, columns, size), F32),
            pltpu.VMEM((2, block_rows, columns, size), F32),
            pltpu.VMEM((2, nbrs, columns, size), F32),
            pltpu.VMEM((columns, size), F32),
            pltpu.VMEM((tiles, columns // 4, size), F32),
            pltpu.VMEM((tiles, columns // 2, size), F32),
            pltpu.VMEM((block_rows, columns, size), F32),
            dma,
            dma((rows, block_rows)),
            dma((rows, block_rows)),
            dma((2, rows, block_rows)),
            dma((2, group)),
            dma((2, block_rows)),
            dma((2, nbrs)),
            dma((rows, nbrs)),
            dma((tiles,)),
            dma((tiles,)),
            dma((tiles,)),
            dma((group,)),
            dma((tiles,)),
            dma((nbrs,)),
            dma((block_rows,)),
        ],
        compiler_params=pltpu.CompilerParams(collective_id=0, has_side_effects=True),
    )(partner_ids, counts, start.T, blocks)
    return basis.T, ritz


def solution(mesh):
    rows, nbrs = mesh.shape["row"], mesh.shape["nbr"]

    def program(blocks, partner_ids, counts, start):
        block_rows = partner_ids.shape[0]
        size, columns = blocks.shape[2], start.shape[1]
        if rows * nbrs <= DIRECT_PEERS and block_rows <= nbrs and size == 128 and 4 * columns == size:
            return direct_body(rows, nbrs, blocks, partner_ids, counts, start)
        return body(blocks, partner_ids, counts, start)

    return jax.shard_map(
        program,
        mesh=mesh,
        in_specs=(
            P(("dom", "row"), "nbr", None, None),
            P(("dom", "row"), "nbr"),
            P(("dom", "row")),
            P(("dom", "row"), None),
        ),
        out_specs=(P(("dom", "row"), None), P("dom", None)),
        check_vma=False,
    )
```

time: 44.9 us -> 38.7 us (0.86)
  Pallas kernels: 42 us -> 35.8 us
    pallas_call x1, Pallas kernels: 42 us -> 35.8 us  [direct_body(): pl.pallas_call(functools.partial(kernel, rows, nbrs), out_shape=(jax.Shap...]
where the time goes in v2:
time: 38.7 us; the launch traced here: 38.5 us
  Pallas kernels  35.8 us (93%)
  local copies, waits for them, and re-layouts  2.04 us (5%)
  between operations  0.65 us (2%)
    pallas_call x1, Pallas kernels, direct_body(): pl.pallas_call(functools.partial(kernel, rows, nbrs), out_shape=(jax.Shap...  35.8 us
    unnamed x4, local copies, waits for them, and re-layouts  2.04 us

profile of v2, /device:TPU:0, one launch (start us, length us, event | category | flops | bytes accessed | tf_op | source)
XLA Modules:
  0.0 38.5 jit_solution(9783854502542121289)
XLA Ops:
  0.6 35.8 %shard_map.59 = (f32[32,384]{1,0:T(8,128)}, f32[32,32]{1,0:T(8,128)}) custom-call(s32[3,3]{1,0:T(4,128)} %ids_ref.1, s32[3]{0:T(128)} %counts_ref.1, f32[32,384]{1,0:T(8,128)} %bitcast.2, f32[3,3,128,128]{3,2,1,0:T(8,128)} %blocks_ref.1), custom_call_target="tpu_custom_call" | custom-call | tf_op jit(solution)/shard_map/pallas_call | solution.py:441
  36.4 0.0 copy-start
  36.4 1.4 %copy.8 = f32[384,32]{0,1:T(8,128)} copy(f32[384,32]{0,1:T(8,128)} %bitcast.3) | data formatting | bytes 98304
  37.8 0.0 copy-done
  37.8 0.6 %copy.9 = f32[32,32]{1,0:T(8,128)} copy(f32[32,32]{1,0:T(8,128)S(1)} %copy-done) | data formatting | bytes 8192
Async XLA Ops:
  36.4 1.4 %copy-start = (f32[32,32]{1,0:T(8,128)S(1)}, f32[32,32]{1,0:T(8,128)}, u32[]{:S(2)}) copy-start(f32[32,32]{1,0:T(8,128)} %get-tuple-element.9) | copy-start | bytes 12292

commit v3 on v2

--- a/solution.py
+++ b/solution.py
@@ -96,10 +96,10 @@
 
 
 def kernel(
-    rows, nbrs, ids_ref, counts_ref, start_ref, blocks_ref, basis_ref, ritz_ref,
+    rows, nbrs, ids_ref, counts_ref, start_ref, blocks_ref, out_ref,
     held, straight, turned, sel, weight, begun, first_image, part, inbox, near_part, near_inbox, total_sum,
     grams, stats, images,
-    blocks_sem, start_send, start_recv, rs_send, rs_recv, near_send, near_recv, ag_send, ag_recv,
+    blocks_sem, start_send, start_recv, relay_send, relay_recv, rs_send, rs_recv, near_send, near_recv, ag_send, ag_recv,
     gram_send, gram_recv, st_send, st_recv, im_send, im_recv,
 ):
     block_rows, slots = ids_ref.shape
@@ -116,6 +116,9 @@
     my_tile = first_tile + my_slot
     whole = (begun, first_image)
     blank = jnp.zeros((columns, size), F32)
+    half, quarter = columns // 2, columns // 4
+    side = lax.rem(my_nbr, 2)
+    partner = my_nbr + 1 - 2 * side
 
     def send(src, dst, send_sem, recv_sem, r, n):
         return pltpu.make_async_remote_copy(
@@ -184,17 +187,46 @@
             out = dot_nn(jnp.concatenate(far + far, axis=1), turned[i], None)
             near_part[step, i] = out[:columns] + out[columns:]
 
+    def half_at(ref, t, h):
+        return ref.at[t, pl.ds(pl.multiple_of(h * half, half), half)]
+
     def start_copy(q, i):
         return send(
-            start_ref.at[:, pl.ds(i * size, size)], begun.at[first_tile + i],
+            start_ref.at[pl.ds(pl.multiple_of(side * half, half), half), pl.ds(i * size, size)],
+            half_at(begun, first_tile + i, side),
             start_send.at[q, i], start_recv.at[my_row, i], q, my_nbr,
         )
 
     def start_wait(q, i):
+        mine = half_at(begun, q * block_rows + i, side)
+        send(mine, mine, start_send.at[q, i], start_recv.at[q, i], q, my_nbr).wait_recv()
+
+    def relay(step, q, i):
+        mine = half_at(whole[step], q * block_rows + i, side)
+        return send(
+            mine, mine, relay_send.at[step, q, i], relay_recv.at[step, q, i], my_row, partner
+        )
+
+    def relay_wait(step, q, i):
+        other = half_at(whole[step], q * block_rows + i, 1 - side)
         send(
-            start_ref.at[:, pl.ds(i * size, size)], begun.at[q * block_rows + i],
-            start_send.at[q, i], start_recv.at[q, i], q, my_nbr,
+            other, other, relay_send.at[step, q, i], relay_recv.at[step, q, i], my_row, partner
         ).wait_recv()
+
+    def each_later(act):
+        for q in range(1, rows):
+            @pl.when(q > my_row)
+            def _():
+                for i in range(block_rows):
+                    act(q, i)
+
+    def pass_on(step, wait):
+        def act(q, i):
+            wait(q, i)
+            relay(step, q, i).start()
+
+        each_later(act)
+        each_later(lambda q, i: relay_wait(step, q, i))
 
     def sum_copy(step, r, n):
         return send(
@@ -274,7 +306,16 @@
             @pl.when(q < my_row)
             def _():
                 for n in range(nbrs):
-                    act(image_copy(q, n))
+                    act(far_copy(q, n))
+
+    def far_copy(q, n):
+        piece = half_at(first_image, my_tile, n % 2)
+        return send(piece, piece, ag_send.at[q, n], ag_recv.at[my_tile], q, n)
+
+    def far_wait(q, i):
+        t = q * block_rows + i
+        mine = half_at(first_image, t, side)
+        send(mine, mine, ag_send.at[0, 0], ag_recv.at[t], my_row, my_nbr).wait_recv()
 
     def gram_copy(t):
         return send(
@@ -294,22 +335,44 @@
             def _():
                 act(t)
 
-    def stats_copy(g):
-        return send(
-            stats.at[my_tile], stats.at[my_tile],
-            st_send.at[g], st_recv.at[my_tile], g // nbrs, g % nbrs,
-        )
-
-    def stats_wait(t):
-        send(
-            stats.at[t], stats.at[t], st_send.at[0], st_recv.at[t], my_row, my_nbr
-        ).wait_recv()
-
-    def each_stats(act):
-        for g in range(group):
-            @pl.when(g != me)
-            def _():
-                act(stats_copy(g))
+    def stats_copy(kind, r, n):
+        return send(
+            stats.at[kind, my_tile], stats.at[kind, my_tile],
+            st_send.at[kind, r, n], st_recv.at[kind, my_tile], r, n,
+        )
+
+    def stats_wait(kind):
+        for t in range(tiles):
+            @pl.when(jnp.logical_or(jnp.logical_not(owner), t != my_tile))
+            def _():
+                send(
+                    stats.at[kind, t], stats.at[kind, t],
+                    st_send.at[kind, 0, 0], st_recv.at[kind, t], my_row, my_nbr,
+                ).wait_recv()
+
+    def each_stats(kind, act):
+        for k in range(rows):
+            r = jnp.where(2 * my_row >= rows, k, rows - 1 - k)
+            for e in range(nbrs):
+                n = lax.rem(my_nbr + nbrs - 1 - e, nbrs)
+                @pl.when(r * nbrs + n != me)
+                def _():
+                    act(stats_copy(kind, r, n))
+
+    def pack(square):
+        packed = square[:quarter]
+        for g in range(1, 4):
+            packed = packed + pltpu.roll(square[g * quarter : (g + 1) * quarter], g * columns, 1)
+        return packed
+
+    def unpack(parts):
+        packed = parts[0]
+        for t in range(1, tiles):
+            packed = packed + parts[t]
+        packed = packed / total
+        return jnp.concatenate(
+            [pltpu.roll(packed, size - g * columns, 1) if g else packed for g in range(4)], axis=0
+        )
 
     def own_copy(e):
         return send(
@@ -339,15 +402,9 @@
     pl.semaphore_wait(barrier, group - 1)
     each_start(begin)
     each_sum(0, begin)
-    for q in range(1, rows):
-        @pl.when(q > my_row)
-        def _():
-            for i in range(block_rows):
-                start_wait(q, i)
+    pass_on(0, start_wait)
     direct(0)
     each_near(0, begin)
-
-    quarter, half = columns // 4, columns // 2
 
     @pl.when(owner)
     def _():
@@ -356,10 +413,7 @@
         near_images(begin)
         far_images(begin)
         gram = dot_nt(tile, jnp.concatenate([tile, blank, blank, blank], axis=0))
-        packed = gram[:quarter]
-        for g in range(1, 4):
-            packed = packed + pltpu.roll(gram[g * quarter : (g + 1) * quarter], g * columns, 1)
-        grams[my_tile] = packed
+        grams[my_tile] = pack(gram)
         each_gram(lambda t: gram_copy(t).start())
 
     for i in range(block_rows):
@@ -368,56 +422,40 @@
             image_wait(first_tile + i)
     transposed(1)
     each_sum(1, begin)
-    for q in range(1, rows):
-        @pl.when(q > my_row)
-        def _():
-            for i in range(block_rows):
-                image_wait(q * block_rows + i)
+    pass_on(1, far_wait)
     direct(1)
     each_near(1, begin)
 
     @pl.when(owner)
     def _():
         each_gram(gram_wait)
-        packed = grams[0]
-        for t in range(1, tiles):
-            packed = packed + grams[t]
-        packed = packed / total
-        gram = jnp.concatenate(
-            [pltpu.roll(packed, size - g * columns, 1) if g else packed for g in range(4)], axis=0
-        )
+        gram = unpack(grams)
         first = inverse_factor(pltpu.roll(gram, columns, 1), columns, size)
         prior = dot_nn(first, first_image[my_tile])
         image = dot_nn(first, gather_sums(1))
         images[my_nbr] = image
-        both = dot_nt(image, jnp.concatenate([image, blank, blank, blank], axis=0))
-        other = dot_nt(prior, jnp.concatenate([blank, image, blank, blank], axis=0))
-        both = both + other
-        stats[my_tile] = both[:half] + pltpu.roll(both[half:], 2 * columns, 1)
-        each_stats(begin)
+        padded = jnp.concatenate([image, blank, blank, blank], axis=0)
+        stats[0, my_tile] = pack(dot_nt(image, padded))
+        each_stats(0, begin)
         for e in range(1, nbrs):
             own_copy(e).start()
-
-    for t in range(tiles):
-        @pl.when(jnp.logical_or(jnp.logical_not(owner), t != my_tile))
-        def _():
-            stats_wait(t)
-    packed = stats[0]
-    for t in range(1, tiles):
-        packed = packed + stats[t]
-    packed = packed / total
-    rest = jnp.concatenate([packed, pltpu.roll(packed, 2 * columns, 1)], axis=0)
-    last = inverse_factor(pltpu.roll(rest, columns, 1), columns, size)
-    ritz_ref[...] = pltpu.roll(rest, size - columns, 1)[:, :columns]
+        stats[1, my_tile] = pack(dot_nt(prior, padded))
+        each_stats(1, begin)
+
+    stats_wait(0)
+    last = inverse_factor(pltpu.roll(unpack(stats.at[0]), columns, 1), columns, size)
     for i in range(block_rows):
         @pl.when(i != my_nbr)
         def _():
             own_wait(i)
     for i in range(block_rows):
-        basis_ref[:, i * size : (i + 1) * size] = dot_nn(last, images[i])
+        out_ref[:, i * size : (i + 1) * size] = dot_nn(last, images[i])
+    stats_wait(1)
+    out_ref[:, block_rows * size :] = unpack(stats.at[1])
 
     each_start(end)
     for step in range(ITERS):
+        each_later(lambda q, i: relay(step, q, i).wait_send())
         each_sum(step, end)
         each_near(step, end)
 
@@ -426,9 +464,16 @@
         near_images(end)
         far_images(end)
         each_gram(lambda t: gram_copy(t).wait_send())
-        each_stats(end)
+        each_stats(0, end)
+        each_stats(1, end)
         for e in range(1, nbrs):
             own_copy(e).wait_send()
+
+
+def part_outputs(joined_ref, basis_ref, ritz_ref):
+    width = basis_ref.shape[1]
+    basis_ref[...] = joined_ref[:, :width]
+    ritz_ref[...] = joined_ref[:, width : width + ritz_ref.shape[1]]
 
 
 def direct_body(rows, nbrs, blocks, partner_ids, counts, start):
@@ -438,22 +483,16 @@
     tiles = block_rows * rows
     group = rows * nbrs
     dma = pltpu.SemaphoreType.DMA
-    basis, ritz = pl.pallas_call(
+    joined = pl.pallas_call(
         functools.partial(kernel, rows, nbrs),
-        out_shape=(
-            jax.ShapeDtypeStruct((columns, block_rows * size), F32),
-            jax.ShapeDtypeStruct((columns, columns), F32),
-        ),
+        out_shape=jax.ShapeDtypeStruct((columns, (block_rows + 1) * size), F32),
         in_specs=[
             pl.BlockSpec(memory_space=pltpu.SMEM),
             pl.BlockSpec(memory_space=pltpu.SMEM),
             pl.BlockSpec(memory_space=pltpu.VMEM),
-            pl.BlockSpec(memory_space=pl.ANY),
+            pl.BlockSpec(memory_space=pltpu.HBM),
         ],
-        out_specs=(
-            pl.BlockSpec(memory_space=pltpu.VMEM),
-            pl.BlockSpec(memory_space=pltpu.VMEM),
-        ),
+        out_specs=pl.BlockSpec(memory_space=pltpu.VMEM),
         scratch_shapes=[
             pltpu.VMEM((block_rows, slots, size, size), F32),
             pltpu.VMEM((block_rows, 2 * size, slots * size), BF16),
@@ -468,11 +507,13 @@
             pltpu.VMEM((2, nbrs, columns, size), F32),
             pltpu.VMEM((columns, size), F32),
             pltpu.VMEM((tiles, columns // 4, size), F32),
-            pltpu.VMEM((tiles, columns // 2, size), F32),
+            pltpu.VMEM((2, tiles, columns // 4, size), F32),
             pltpu.VMEM((block_rows, columns, size), F32),
             dma,
             dma((rows, block_rows)),
             dma((rows, block_rows)),
+            dma((2, rows, block_rows)),
+            dma((2, rows, block_rows)),
             dma((2, rows, block_rows)),
             dma((2, group)),
             dma((2, block_rows)),
@@ -481,13 +522,25 @@
             dma((tiles,)),
             dma((tiles,)),
             dma((tiles,)),
-            dma((group,)),
-            dma((tiles,)),
+            dma((2, rows, nbrs)),
+            dma((2, tiles)),
             dma((nbrs,)),
             dma((block_rows,)),
         ],
         compiler_params=pltpu.CompilerParams(collective_id=0, has_side_effects=True),
     )(partner_ids, counts, start.T, blocks)
+    basis, ritz = pl.pallas_call(
+        part_outputs,
+        out_shape=(
+            jax.ShapeDtypeStruct((columns, block_rows * size), F32),
+            jax.ShapeDtypeStruct((columns, columns), F32),
+        ),
+        in_specs=[pl.BlockSpec(memory_space=pltpu.VMEM)],
+        out_specs=(
+            pl.BlockSpec(memory_space=pltpu.VMEM),
+            pl.BlockSpec(memory_space=pltpu.VMEM),
+        ),
+    )(joined)
     return basis.T, ritz
 
 
@@ -497,7 +550,7 @@
     def program(blocks, partner_ids, counts, start):
         block_rows = partner_ids.shape[0]
         size, columns = blocks.shape[2], start.shape[1]
-        if rows * nbrs <= DIRECT_PEERS and block_rows <= nbrs and size == 128 and 4 * columns == size:
+        if rows * nbrs <= DIRECT_PEERS and block_rows <= nbrs and nbrs % 2 == 0 and size == 128 and 4 * columns == size:
             return direct_body(rows, nbrs, blocks, partner_ids, counts, start)
         return body(blocks, partner_ids, counts, start)
 

time: 38.7 us -> 37.3 us (0.964)
  local copies, waits for them, and re-layouts: 2.04 us -> 0 us
  Pallas kernels: 35.8 us -> 36.3 us
    unnamed x4 -> x0, local copies, waits for them, and re-layouts: 2.04 us -> none
    pallas_call x1 -> x2, Pallas kernels: 35.8 us -> 36.3 us  [the longest x1 34.9 us: direct_body(): pl.pallas_call(functools.partial(kernel, rows, nbrs), out_shape=jax.Shape...]
where the time goes in v3:
time: 37.3 us; the launch traced here: 37 us
  Pallas kernels  36.3 us (97%)
  between operations  0.64 us (2%)
    pallas_call x1, Pallas kernels, direct_body(): pl.pallas_call(functools.partial(kernel, rows, nbrs), out_shape=jax.Shape...  34.9 us
    pallas_call x1, Pallas kernels, direct_body(): pl.pallas_call(part_outputs, out_shape=(jax.ShapeDtypeStruct((columns, bl...  1.47 us

profile of v3, /device:TPU:0, one launch (start us, length us, event | category | flops | bytes accessed | tf_op | source)
XLA Modules:
  0.0 37.0 jit_solution(12378898485541173237)
XLA Ops:
  0.6 34.9 %shard_map.59.joined_ref = f32[32,512]{1,0:T(8,128)} custom-call(s32[3,3]{1,0:T(4,128)} %ids_ref.1, s32[3]{0:T(128)} %counts_ref.1, f32[32,384]{1,0:T(8,128)} %bitcast.2, f32[3,3,128,128]{3,2,1,0:T(8,128)} %blocks_ref.1), custom_call_target="tpu_custom_call" | custom-call | tf_op jit(solution)/shard_map/pallas_call | solution.py:486
  35.5 1.5 %shard_map.60 = (f32[32,384]{1,0:T(8,128)}, f32[32,32]{1,0:T(8,128)}) custom-call(f32[32,512]{1,0:T(8,128)} %shard_map.59.joined_ref), custom_call_target="tpu_custom_call" | custom-call | tf_op jit(solution)/shard_map/pallas_call | solution.py:532

commit v4 on v3

--- a/solution.py
+++ b/solution.py
@@ -97,9 +97,9 @@
 
 def kernel(
     rows, nbrs, ids_ref, counts_ref, start_ref, blocks_ref, out_ref,
-    held, straight, turned, sel, weight, begun, first_image, part, inbox, near_part, near_inbox, total_sum,
+    held, straight, turned, sel, weight, begun, first_image, part, pair_in, pair_sum, inbox, near_part, near_inbox, total_sum,
     grams, stats, images,
-    blocks_sem, start_send, start_recv, relay_send, relay_recv, rs_send, rs_recv, near_send, near_recv, ag_send, ag_recv,
+    blocks_sem, start_send, start_recv, relay_send, relay_recv, pair_send, pair_recv, rs_send, rs_recv, near_send, near_recv, ag_send, ag_recv,
     gram_send, gram_recv, st_send, st_recv, im_send, im_recv,
 ):
     block_rows, slots = ids_ref.shape
@@ -230,18 +230,44 @@
 
     def sum_copy(step, r, n):
         return send(
-            part.at[step, r * block_rows + n], inbox.at[step, me],
+            pair_sum.at[step, r * block_rows + n], inbox.at[step, me],
             rs_send.at[step, r, n], rs_recv.at[step, me], r, n,
         )
 
     def sum_wait(step, r, n):
         send(
-            part.at[step, my_tile], inbox.at[step, r * nbrs + n],
+            pair_sum.at[step, my_tile], inbox.at[step, r * nbrs + n],
             rs_send.at[step, 0, 0], rs_recv.at[step, r * nbrs + n], r, n,
         ).wait_recv()
 
+    def pair_copy(step, r):
+        here = pl.ds(r * block_rows, block_rows)
+        theirs = pl.ds(pl.multiple_of((1 - side) * half, half), half)
+        return send(
+            part.at[step, here, theirs], pair_in.at[step, here],
+            pair_send.at[step, r], pair_recv.at[step, r], my_row, partner,
+        )
+
+    def each_pair(step, act):
+        for r in reversed(range(rows)):
+            @pl.when(r >= my_row)
+            def _():
+                act(r)
+
+    def send_sums(step):
+        each_pair(step, lambda r: pair_copy(step, r).start())
+
+        def finish(r):
+            pair_copy(step, r).wait_recv()
+            for t in range(r * block_rows, (r + 1) * block_rows):
+                own = part[step, t, pl.ds(pl.multiple_of(side * half, half), half)]
+                pair_sum[step, t] = own + pair_in[step, t]
+
+        each_pair(step, finish)
+        each_sum(step, begin)
+
     def each_sum(step, act):
-        for r in range(rows):
+        for r in reversed(range(rows)):
             for n in range(block_rows):
                 @pl.when(jnp.logical_and(r >= my_row, r * nbrs + n != me))
                 def _():
@@ -266,20 +292,25 @@
                 act(near_copy(step, i))
 
     def gather_sums(step):
-        total_sum[...] = part[step, my_tile] + near_part[step, my_slot]
-        for q in range(rows - 1):
+        total_sum[...] = near_part[step, my_slot]
+        inbox[step, me] = pair_sum[step, my_tile]
+
+        def add(q):
+            for h in range(2):
+                summed = inbox[step, q * nbrs + h]
+                for n in range(h + 2, nbrs, 2):
+                    summed = summed + inbox[step, q * nbrs + n]
+                total_sum[h * half : (h + 1) * half, :] += summed
+
+        for e in range(1, nbrs):
+            sum_wait(step, my_row, lax.rem(my_nbr + e, nbrs))
+        add(my_row)
+        for q in reversed(range(rows - 1)):
             @pl.when(q < my_row)
             def _():
                 for n in range(nbrs):
                     sum_wait(step, q, n)
-                summed = inbox[step, q * nbrs]
-                for n in range(1, nbrs):
-                    summed = summed + inbox[step, q * nbrs + n]
-                total_sum[...] += summed
-        for e in range(1, nbrs):
-            n = lax.rem(my_nbr + e, nbrs)
-            sum_wait(step, my_row, n)
-            total_sum[...] += inbox[step, my_row * nbrs + n]
+                add(q)
         for e in range(1, nbrs):
             n = lax.rem(my_nbr + e, nbrs)
             near_wait(step, n)
@@ -401,7 +432,7 @@
     transposed(0)
     pl.semaphore_wait(barrier, group - 1)
     each_start(begin)
-    each_sum(0, begin)
+    send_sums(0)
     pass_on(0, start_wait)
     direct(0)
     each_near(0, begin)
@@ -421,7 +452,7 @@
         def _():
             image_wait(first_tile + i)
     transposed(1)
-    each_sum(1, begin)
+    send_sums(1)
     pass_on(1, far_wait)
     direct(1)
     each_near(1, begin)
@@ -456,6 +487,7 @@
     each_start(end)
     for step in range(ITERS):
         each_later(lambda q, i: relay(step, q, i).wait_send())
+        each_pair(step, lambda r: pair_copy(step, r).wait_send())
         each_sum(step, end)
         each_near(step, end)
 
@@ -502,7 +534,9 @@
             pltpu.VMEM((tiles, columns, size), F32),
             pltpu.VMEM((tiles, columns, size), F32),
             pltpu.VMEM((2, tiles, columns, size), F32),
-            pltpu.VMEM((2, group, columns, size), F32),
+            pltpu.VMEM((2, tiles, columns // 2, size), F32),
+            pltpu.VMEM((2, tiles, columns // 2, size), F32),
+            pltpu.VMEM((2, group, columns // 2, size), F32),
             pltpu.VMEM((2, block_rows, columns, size), F32),
             pltpu.VMEM((2, nbrs, columns, size), F32),
             pltpu.VMEM((columns, size), F32),
@@ -514,6 +548,8 @@
             dma((rows, block_rows)),
             dma((2, rows, block_rows)),
             dma((2, rows, block_rows)),
+            dma((2, rows)),
+            dma((2, rows)),
             dma((2, rows, block_rows)),
             dma((2, group)),
             dma((2, block_rows)),

time: 37.3 us -> 35.7 us (0.957)
  Pallas kernels: 36.3 us -> 34.8 us
    pallas_call x1, Pallas kernels: 34.9 us -> 33.4 us  [direct_body(): pl.pallas_call(functools.partial(kernel, rows, nbrs), out_shape=jax.Shape...]
where the time goes in v4:
time: 35.7 us; the launch traced here: 35.5 us
  Pallas kernels  34.8 us (97%)
  between operations  0.64 us (2%)
    pallas_call x1, Pallas kernels, direct_body(): pl.pallas_call(functools.partial(kernel, rows, nbrs), out_shape=jax.Shape...  33.4 us
    pallas_call x1, Pallas kernels, direct_body(): pl.pallas_call(part_outputs, out_shape=(jax.ShapeDtypeStruct((columns, bl...  1.47 us

profile of v4, /device:TPU:0, one launch (start us, length us, event | category | flops | bytes accessed | tf_op | source)
XLA Modules:
  0.0 35.5 jit_solution(4841534440979052856)
XLA Ops:
  0.6 33.4 %shard_map.59.joined_ref = f32[32,512]{1,0:T(8,128)} custom-call(s32[3,3]{1,0:T(4,128)} %ids_ref.1, s32[3]{0:T(128)} %counts_ref.1, f32[32,384]{1,0:T(8,128)} %bitcast.2, f32[3,3,128,128]{3,2,1,0:T(8,128)} %blocks_ref.1), custom_call_target="tpu_custom_call" | custom-call | tf_op jit(solution)/shard_map/pallas_call | solution.py:518
  34.0 1.5 %shard_map.60 = (f32[32,384]{1,0:T(8,128)}, f32[32,32]{1,0:T(8,128)}) custom-call(f32[32,512]{1,0:T(8,128)} %shard_map.59.joined_ref), custom_call_target="tpu_custom_call" | custom-call | tf_op jit(solution)/shard_map/pallas_call | solution.py:568
